TPU v7x, 512 devices: a whole 4x4x16 slice. The times are simulated.
512 devices in a mesh: tile: 32 (over z, core), help: 4 (over x), dp: 4 (over y).
Axes of the slice: x: 4, y: 4, z: 16, core: 2. Of those that a mesh axis runs over, the one named last changes fastest.
Arguments:
- tokens: bfloat16 [4, 262144, 256], P('dp', ('tile', 'help')), may hold values from -6 to 6
- d_out: bfloat16 [4, 262144, 256], P('dp', ('tile', 'help')), may hold values from -6 to 6
- gain: float32 [256], replicated, may hold values from 0.5 to 1.5
- w_qkv: bfloat16 [256, 768], replicated, may hold values from -10 to 10
- w_out: bfloat16 [256, 256], replicated, may hold values from -0.375 to 0.375
- counts: int32 [4, 1024], P('dp', 'tile'), may hold values from 0 to 256, as said below
Outputs:
- grad_tokens: bfloat16 [4, 262144, 256], P('dp', ('tile', 'help'))
- grad_qkv: float32 [256, 768], replicated
- grad_out: float32 [256, 256], replicated
- grad_gain: float32 [256], replicated
Inputs may be any that keep to these rules, and one draw needn't show every extreme that they name: `counts`: entry s * 8 + w of a slab, with s = tile index * 4 + help index, is the active voxel count of window slot w of device s. A device's active windows come first. Of the two devices of a tile whose help indices differ by 2, one holds 8 active windows and the other 4. Every active window holds 1 to 256 voxels, and some window is full in every draw.
All inputs are finite; a program needn't handle non-finite values.
Results may differ from a plain program's by a relative error of at most 0.005.
The roundings to bfloat16 on the way count: a program that leaves them out, or rounds other values in their place, can miss the bound.
Values may be sent and summed in bfloat16 or wider, within the bound.
No kernel may reach another device: no remote copies, remote signals or barrier semaphores. Data moves between devices by JAX's collectives and lax.ppermute only.
A program may use at most 64 MiB of HBM per device.

v0:
```python
import math

import jax
import jax.numpy as jnp
from jax import lax
from jax.sharding import PartitionSpec as P

HEADS = 8
WIN = 256
WKEEP = 6


def window_grads(window_input, window_upstream, active, gain, w_qkv, w_out):
    features = window_input.shape[-1]
    head_dim = features // HEADS
    factor = 1.0 / math.sqrt(head_dim)
    tokens_f = window_input.astype(jnp.float32)
    center = tokens_f - jnp.mean(tokens_f, axis=-1, keepdims=True)
    inverse = lax.rsqrt(jnp.mean(center * center, axis=-1, keepdims=True) + 1e-05)
    normed = center * inverse
    hidden = (normed * gain).astype(jnp.bfloat16)
    projected = jnp.dot(hidden, w_qkv, preferred_element_type=jnp.float32).astype(jnp.bfloat16)
    query_rows = projected[:, :features].reshape(-1, HEADS, head_dim)
    key_rows = projected[:, features : 2 * features].reshape(-1, HEADS, head_dim)
    value_rows = projected[:, 2 * features :].reshape(-1, HEADS, head_dim)
    scores = (
        jnp.einsum("qhc,khc->hqk", query_rows, key_rows, preferred_element_type=jnp.float32)
        * factor
    )
    scores = jnp.where(active[None, None, :], scores, -1e30)
    highest = jnp.max(scores, axis=-1, keepdims=True)
    exponent = jnp.exp(scores - highest)
    probability = exponent / jnp.sum(exponent, axis=-1, keepdims=True)
    prob_half = probability.astype(jnp.bfloat16)
    attended = (
        jnp.einsum("hqk,khc->qhc", prob_half, value_rows, preferred_element_type=jnp.float32)
        .astype(jnp.bfloat16)
        .reshape(-1, features)
    )
    grad_attn = jnp.einsum(
        "td,ed->te", window_upstream, w_out, preferred_element_type=jnp.float32
    ).astype(jnp.bfloat16)
    grad_heads = grad_attn.reshape(-1, HEADS, head_dim)
    grad_prob = jnp.einsum(
        "qhc,khc->hqk", grad_heads, value_rows, preferred_element_type=jnp.float32
    )
    grad_value = jnp.einsum(
        "hqk,qhc->khc", prob_half, grad_heads, preferred_element_type=jnp.float32
    ).astype(jnp.bfloat16)
    grad_score = (
        probability
        * (grad_prob - jnp.sum(probability * grad_prob, axis=-1, keepdims=True))
        * factor
    ).astype(jnp.bfloat16)
    grad_query = jnp.einsum(
        "hqk,khc->qhc", grad_score, key_rows, preferred_element_type=jnp.float32
    ).astype(jnp.bfloat16)
    grad_key = jnp.einsum(
        "hqk,qhc->khc", grad_score, query_rows, preferred_element_type=jnp.float32
    ).astype(jnp.bfloat16)
    grad_proj = jnp.concatenate(
        [
            grad_query.reshape(-1, features),
            grad_key.reshape(-1, features),
            grad_value.reshape(-1, features),
        ],
        axis=-1,
    )
    grad_hidden = jnp.einsum("te,de->td", grad_proj, w_qkv, preferred_element_type=jnp.float32)
    part_gain = jnp.sum(grad_hidden * normed, axis=0)
    part_qkv = jnp.einsum("td,te->de", hidden, grad_proj, preferred_element_type=jnp.float32)
    part_out = jnp.einsum(
        "td,te->de", attended, window_upstream, preferred_element_type=jnp.float32
    )
    grad_norm = grad_hidden * gain
    grad_input = inverse * (
        grad_norm
        - jnp.mean(grad_norm, axis=-1, keepdims=True)
        - normed * jnp.mean(grad_norm * normed, axis=-1, keepdims=True)
    )
    grad_full = window_upstream.astype(jnp.float32) + grad_input
    grad_rows = jnp.where(active[:, None], grad_full, 0.0).astype(jnp.bfloat16)
    return (grad_rows, part_gain, part_qkv, part_out)


def per_device(tokens, d_out, gain, w_qkv, w_out, counts):
    features = tokens.shape[2]
    slot_count = tokens.shape[1] // WIN
    group_size = lax.axis_size("tile") * lax.axis_size("help")
    help_index = lax.axis_index("help")
    own_counts = lax.dynamic_slice_in_dim(counts[0], help_index * slot_count, slot_count)
    block_in = tokens[0].reshape(slot_count, WIN, features)
    block_up = d_out[0].reshape(slot_count, WIN, features)
    slot_ids = jnp.arange(WIN, dtype=jnp.int32)
    start_sums = (
        jnp.zeros((features,), jnp.float32),
        jnp.zeros((features, 3 * features), jnp.float32),
        jnp.zeros((features, features), jnp.float32),
    )

    def window_step(carry, block):
        block_input, block_upstream, block_mask = block
        grad_rows, part_gain, part_qkv, part_out = window_grads(
            block_input, block_upstream, block_mask, gain, w_qkv, w_out
        )
        return ((carry[0] + part_gain, carry[1] + part_qkv, carry[2] + part_out), grad_rows)

    work_in = block_in
    work_up = block_up
    active = slot_ids[None, :] < own_counts[:, None]
    work_in = jnp.where(active[:, :, None], work_in, 0)
    work_up = jnp.where(active[:, :, None], work_up, 0)
    totals, grad_local = lax.scan(window_step, start_sums, (work_in, work_up, active))
    gain_part, qkv_part, out_part = totals
    total_gain, total_qkv, total_out = lax.psum(
        (gain_part, qkv_part, out_part), ("tile", "help", "dp")
    )
    factor = 1.0 / math.sqrt(lax.axis_size("dp") * group_size * WKEEP * WIN)
    grad_tokens = grad_local.reshape(slot_count * WIN, features)
    return (grad_tokens[None], total_qkv * factor, total_out * factor, total_gain * factor)


def solution(mesh):
    in_specs = (
        P("dp", ("tile", "help"), None),
        P("dp", ("tile", "help"), None),
        P(),
        P(),
        P(),
        P("dp", "tile"),
    )
    out_specs = (P("dp", ("tile", "help"), None), P(), P(), P())
    return jax.shard_map(
        per_device, mesh=mesh, in_specs=in_specs, out_specs=out_specs, check_vma=False
    )
```

profile of v0, /device:TPU:1, one launch (start us, length us, event | category | flops | bytes accessed | tf_op | source)
XLA Modules:
  0.0 692.7 jit_solution(4237619867928675163)
XLA Ops:
  8.5 2.8 broadcast_select_fusion
  11.4 190.1 %while.18 = (s32[]{:T(128)}, f32[256]{0:T(256)}, f32[256,768]{1,0:T(8,128)S(1)}, f32[256,256]{1,0:T(8,128)}, bf16[8,256,256]{2,1,0:T(8,128)(2,1)}, /*index=5*/bf...) while((s32[]{:T(128)}, f32[256]{0:T(256)}, ...), condition=%wide.region_9.10_spmd.clone.clone, body=%wide.region_0.9_spmd.clone.sunk.clone | while | flops 587797760 | bytes 32623524 | solution.py:113
  11.4 1.0 constant_dynamic-slice_fusion.4
  14.5 1.7 copy.53
  16.1 0.8 copy.54
  17.6 3.8 fusion.150
  21.4 3.1 fusion.153
  24.5 3.8 fusion.152
  28.3 2.1 convolution_convert_fusion.14
  31.9 1.9 convolution_convert_fusion.15
  35.1 1.0 constant_dynamic-slice_fusion.4
  38.3 1.7 copy.53
  41.3 3.8 fusion.150
  45.1 3.1 fusion.153
  48.3 3.8 fusion.152
  52.0 2.1 convolution_convert_fusion.14
  55.7 1.9 convolution_convert_fusion.15
  58.9 1.0 constant_dynamic-slice_fusion.4
  62.0 1.7 copy.53
  65.1 3.8 fusion.150
  68.9 3.1 fusion.153
  72.0 3.8 fusion.152
  75.8 2.1 convolution_convert_fusion.14
  79.4 1.9 convolution_convert_fusion.15
  82.6 1.0 constant_dynamic-slice_fusion.4
  85.8 1.7 copy.53
  88.9 3.8 fusion.150
  92.6 3.1 fusion.153
  95.8 3.8 fusion.152
  99.5 2.1 convolution_convert_fusion.14
  103.2 1.9 convolution_convert_fusion.15
  106.4 1.0 constant_dynamic-slice_fusion.4
  109.5 1.7 copy.53
  112.6 3.8 fusion.150
  116.4 3.1 fusion.153
  119.5 3.8 fusion.152
  123.3 2.1 convolution_convert_fusion.14
  127.0 1.9 convolution_convert_fusion.15
  130.1 1.0 constant_dynamic-slice_fusion.4
  133.3 1.7 copy.53
  136.4 3.8 fusion.150
  140.2 3.1 fusion.153
  143.3 3.8 fusion.152
  147.0 2.1 convolution_convert_fusion.14
  150.7 1.9 convolution_convert_fusion.15
  153.9 1.0 constant_dynamic-slice_fusion.4
  157.0 1.7 copy.53
  160.1 3.8 fusion.150
  163.9 3.1 fusion.153
  167.0 3.8 fusion.152
  170.8 2.1 convolution_convert_fusion.14
  174.5 1.9 convolution_convert_fusion.15
  177.7 1.0 constant_dynamic-slice_fusion.4
  180.8 1.7 copy.53
  183.9 3.8 fusion.150
  187.7 3.1 fusion.153
  190.8 3.8 fusion.152
  194.5 2.1 convolution_convert_fusion.14
  198.2 1.9 convolution_convert_fusion.15
  201.4 0.9 copy-done.1
  202.3 111.7 %psum.23 = f32[256]{0:T(256)S(1)} all-reduce(f32[256]{0:T(256)} %get-tuple-element.330), channel_id=1, replica_groups=mesh['tile'=32,'help'=4,'dp'=4] {'tile','help','dp'}, use_global_device_ids=true, to_apply=%region_12.13 | all-reduce | flops 256 | bytes 2048 | tf_op jit(solution)/shard_map/psum | solution.py:115
  314.6 367.5 %all-reduce.3.cloned.1.call-done = (f32[256,768]{1,0:T(8,128)}, f32[256,256]{1,0:T(8,128)}) async-done(((f32[256,768]{1,0:T(8,128)}, f32[256,256]{1,0:T(8,128)}), (f32[256,768]{1,0:T(8,128)}, f32[256,256]{1,0:T(8,128)})) %all-reduce.3.cloned.1.call-update) | async-done | bytes 1048592 | tf_op jit(solution)/shard_map/psum | solution.py:115
  682.1 2.1 broadcast_multiply_fusion.3
  684.2 1.7 broadcast_multiply_fusion.4
  (353 shorter events, 51.3 us)
Async XLA Ops:
  7.2 674.9 %all-reduce.3.cloned.1.call-start = ((), (), s32[]{:S(2)}) async-start(), calls=%async_computation | async-start | bytes 2097152 | tf_op jit(solution)/shard_map/psum | solution.py:115
  8.5 2.8 copy-start.2
  8.5 2.8 copy-start.6
  8.5 2.8 copy-start.9
  17.6 3.8 copy-start.10
  28.3 2.1 copy-start.3
  28.3 2.1 copy-start.8
  30.3 1.6 copy-start.14
  31.9 2.0 copy-start.4
  33.9 1.2 copy-start.7
  34.1 0.7 copy-start.5
  41.3 3.8 copy-start.10
  52.0 2.1 copy-start.3
  52.0 2.1 copy-start.8
  54.1 1.6 copy-start.14
  55.7 2.0 copy-start.4
  57.6 0.7 copy-start.12
  57.6 1.2 copy-start.7
  57.9 0.7 copy-start.5
  65.1 3.8 copy-start.10
  75.8 2.1 copy-start.3
  75.8 2.1 copy-start.8
  77.9 1.6 copy-start.14
  79.4 2.0 copy-start.4
  81.4 1.2 copy-start.7
  81.6 0.7 copy-start.5
  88.9 3.8 copy-start.10
  99.5 2.1 copy-start.3
  99.5 2.1 copy-start.8
  101.6 1.6 copy-start.14
  103.2 2.0 copy-start.4
  105.1 0.7 copy-start.12
  105.1 1.2 copy-start.7
  105.4 0.7 copy-start.5
  112.6 3.8 copy-start.10
  123.3 2.1 copy-start.3
  123.3 2.1 copy-start.8
  125.4 1.6 copy-start.14
  126.9 2.0 copy-start.4
  128.9 1.2 copy-start.7
  129.2 0.7 copy-start.5
  136.4 3.8 copy-start.10
  147.0 2.1 copy-start.3
  147.0 2.1 copy-start.8
  149.1 1.6 copy-start.14
  150.7 2.0 copy-start.4
  152.6 0.7 copy-start.12
  152.7 1.2 copy-start.7
  152.9 0.7 copy-start.5
  160.1 3.8 copy-start.10
  170.8 2.1 copy-start.3
  170.8 2.1 copy-start.8
  172.9 1.6 copy-start.14
  174.5 2.0 copy-start.4
  176.4 1.2 copy-start.7
  176.7 0.7 copy-start.5
  183.9 3.8 copy-start.10
  194.5 2.1 copy-start.3
  194.5 2.1 copy-start.8
  196.6 1.6 copy-start.14
  198.2 2.0 copy-start.4
  200.2 1.2 copy-start.7
  200.4 0.7 copy-start.5
  201.4 0.9 copy-start.1
  (22 other events, 13.9 us)
Sparse Core Ops, SparseCore 0:
  202.4 479.6 all-reduce.2
where the time goes:
time: 695 us; the launch traced here: 693 us
  waiting for transfers between devices  368 us (53%)
  matrix products  133 us (19%)
  blocking collectives  112 us (16%)
  local copies, waits for them, and re-layouts  54.2 us (8%)
  between operations  14.1 us (2%)
  other arithmetic  10 us (1%)
    psum x1, waiting for transfers between devices, per_device(): lax.psum((gain_part, qkv_part, out_part), ('tile', 'help', 'dp'))  368 us
    psum x1, blocking collectives, per_device(): lax.psum((gain_part, qkv_part, out_part), ('tile', 'help', 'dp'))  112 us
    sub x8, matrix products, window_grads(): exponent = jnp.exp(scores - highest)  30.3 us
    dot_general x8, matrix products, window_grads(): jnp.einsum('hqk,qhc->khc', grad_score, query_rows, preferred_element_type...  30 us
    dot_general x8, matrix products, window_grads(): jnp.einsum('hqk,khc->qhc', grad_score, key_rows, preferred_element_type=j...  24.9 us
    dot_general x8, matrix products, window_grads(): jnp.einsum('hqk,qhc->khc', prob_half, grad_heads, preferred_element_type=...  16.5 us
    dot_general x8, matrix products, window_grads(): jnp.einsum('hqk,khc->qhc', prob_half, value_rows, preferred_element_type=...  15.5 us
    dynamic_slice x32, local copies, waits for them, and re-layouts, per_device(): lax.scan(window_step, start_sums, (work_in, work_up, active))  14.9 us
  transfers between devices with their start and end apart: 1, of which 1 were waited for; matrix products, arithmetic and copies ran while one was open for 0% of the time, Pallas kernels for 0%

commit v1 on v0

v1 whole, which is shorter than its diff:
```python
import functools
import math

import jax
import jax.numpy as jnp
from jax import lax
from jax.experimental import pallas as pl
from jax.experimental.pallas import tpu as pltpu
from jax.sharding import Mesh
from jax.sharding import PartitionSpec as P

HEADS = 8
WIN = 256
WKEEP = 6
LANES = 128
ROW_STEP = 64
PIECES = 32
PIECE_ROWS = 64
PIECE_PAD = 80


def dot_nn(a, b):
    return jnp.dot(a, b, preferred_element_type=jnp.float32)


def dot_nt(a, b):
    return lax.dot_general(a, b, (((1,), (1,)), ((), ())), preferred_element_type=jnp.float32)


def window_rows(rows, count, x_ref, u_ref, gain, wqkv_ref, wout_ref, qkv_ref, out_ref, gsum_ref, g_ref):
    features = x_ref.shape[-1]
    head_dim = features // HEADS
    per_tile = LANES // head_dim
    factor = 1.0 / math.sqrt(head_dim)
    log_factor = factor * math.log2(math.e)
    half = jnp.bfloat16
    active = lax.broadcasted_iota(jnp.int32, (rows, 1), 0) < count
    tokens = jnp.where(active, x_ref[0, :rows, :].astype(jnp.float32), 0.0)
    upstream = jnp.where(active, u_ref[0, :rows, :].astype(jnp.float32), 0.0)
    upstream_half = upstream.astype(half)
    center = tokens - jnp.mean(tokens, axis=-1, keepdims=True)
    inverse = lax.rsqrt(jnp.mean(center * center, axis=-1, keepdims=True) + 1e-05)
    normed = center * inverse
    hidden = (normed * gain).astype(half)
    queries = dot_nn(hidden, wqkv_ref[:, :features]).astype(half)
    keys = dot_nn(hidden, wqkv_ref[:, features : 2 * features]).astype(half)
    values = dot_nn(hidden, wqkv_ref[:, 2 * features :]).astype(half)
    grad_attn = dot_nt(upstream_half, wout_ref[...]).astype(half)
    hidden_t = hidden.T
    keys_t = keys.T
    values_t = values.T
    lane = lax.broadcasted_iota(jnp.int32, (rows, LANES), 1) // head_dim
    zero = jnp.zeros((), half)

    def masked(array, head):
        tile, place = divmod(head, per_tile)
        block = array[:, tile * LANES : (tile + 1) * LANES]
        return jnp.where(lane == place, block, zero)

    def tile_of(array, head):
        tile = head // per_tile
        return array[:, tile * LANES : (tile + 1) * LANES]

    def products(head):
        scores = dot_nt(masked(keys, head), tile_of(queries, head))
        grad_prob = dot_nt(masked(values, head), tile_of(grad_attn, head))
        return scores, grad_prob

    attended_parts, query_parts = [], []
    key_tiles, value_tiles = [], []
    ready = products(0)
    for head in range(HEADS):
        scores, grad_prob = ready
        if head + 1 < HEADS:
            ready = products(head + 1)
        scores = jnp.where(active, scores, -1e30)
        highest = jnp.max(scores, axis=0, keepdims=True)
        exponent = jnp.exp2((scores - highest) * log_factor)
        probability = exponent * (1.0 / jnp.sum(exponent, axis=0, keepdims=True))
        prob_half = probability.astype(half)
        row_sum = jnp.sum(probability * grad_prob, axis=0, keepdims=True)
        grad_score = (probability * (grad_prob - row_sum) * factor).astype(half)
        span = slice(head * head_dim, (head + 1) * head_dim)
        attended_parts.append(dot_nn(values_t[span, :], prob_half).astype(half))
        query_parts.append(dot_nn(keys_t[span, :], grad_score).astype(half))
        value_part = dot_nn(prob_half, masked(grad_attn, head))
        key_part = dot_nn(grad_score, masked(queries, head))
        if head % per_tile == 0:
            value_tiles.append(value_part)
            key_tiles.append(key_part)
        else:
            value_tiles[-1] = value_tiles[-1] + value_part
            key_tiles[-1] = key_tiles[-1] + key_part
    attended_t = jnp.concatenate(attended_parts, axis=0)
    grad_query = jnp.concatenate(query_parts, axis=0).T
    grad_key = jnp.concatenate(key_tiles, axis=1).astype(half)
    grad_value = jnp.concatenate(value_tiles, axis=1).astype(half)
    grad_proj = jnp.concatenate([grad_query, grad_key, grad_value], axis=1)
    grad_hidden = dot_nt(grad_proj, wqkv_ref[...])
    qkv_ref[...] += dot_nn(hidden_t, grad_proj)
    out_ref[...] += dot_nn(attended_t, upstream_half)
    product = grad_hidden * normed
    gsum_ref[...] += jnp.sum(product, axis=0, keepdims=True)
    grad_norm = grad_hidden * gain
    mean_one = jnp.mean(grad_norm, axis=-1, keepdims=True)
    mean_two = jnp.mean(grad_norm * normed, axis=-1, keepdims=True)
    grad_input = inverse * (grad_norm - mean_one - normed * mean_two)
    g_ref[0, :rows, :] = jnp.where(active, upstream + grad_input, 0.0).astype(half)
    if rows < WIN:
        g_ref[0, rows:, :] = jnp.zeros((WIN - rows, features), half)


def kernel(counts_ref, x_ref, u_ref, gain_ref, wqkv_ref, wout_ref, g_ref, send_ref, qkv_ref, out_ref, gsum_ref):
    step = pl.program_id(0)
    features = x_ref.shape[-1]

    @pl.when(step == 0)
    def _():
        qkv_ref[...] = jnp.zeros_like(qkv_ref)
        out_ref[...] = jnp.zeros_like(out_ref)
        gsum_ref[...] = jnp.zeros_like(gsum_ref)

    count = counts_ref[step]

    @pl.when(count == 0)
    def _():
        g_ref[...] = jnp.zeros_like(g_ref)

    for rows in range(ROW_STEP, WIN + 1, ROW_STEP):
        @pl.when(jnp.logical_and(count > rows - ROW_STEP, count <= rows))
        def _(rows=rows):
            window_rows(
                rows, count, x_ref, u_ref, gain_ref[...], wqkv_ref, wout_ref, qkv_ref, out_ref, gsum_ref, g_ref
            )

    @pl.when(step == pl.num_programs(0) - 1)
    def _():
        extra = PIECE_PAD - PIECE_ROWS
        per_column = features // PIECE_ROWS
        for piece in range(PIECES):
            column, part = divmod(piece, per_column)
            source = qkv_ref if column < 3 * features // LANES else out_ref
            column = column % (3 * features // LANES)
            block = source[
                part * PIECE_ROWS : (part + 1) * PIECE_ROWS, column * LANES : (column + 1) * LANES
            ]
            send_ref[piece, :PIECE_ROWS, :] = block.astype(send_ref.dtype)
            tail = jnp.zeros((extra, LANES), jnp.float32)
            if piece < features // LANES:
                tail = tail + jnp.where(
                    lax.broadcasted_iota(jnp.int32, (extra, LANES), 0) == 0,
                    gsum_ref[:, piece * LANES : (piece + 1) * LANES],
                    0.0,
                )
            send_ref[piece, PIECE_ROWS:, :] = tail.astype(send_ref.dtype)


def local_grads(own_counts, tokens, d_out, gain, w_qkv, w_out):
    slots, features = own_counts.shape[0], gain.shape[-1]

    def window_map(step, counts):
        return (jnp.where(counts[step] > 0, step, 0), 0, 0)

    return pl.pallas_call(
        kernel,
        grid_spec=pltpu.PrefetchScalarGridSpec(
            num_scalar_prefetch=1,
            grid=(slots,),
            in_specs=[
                pl.BlockSpec((1, WIN, features), lambda step, counts: (step, 0, 0)),
                pl.BlockSpec((1, WIN, features), lambda step, counts: (step, 0, 0)),
                pl.BlockSpec((1, features), lambda step, counts: (0, 0)),
                pl.BlockSpec((features, 3 * features), lambda step, counts: (0, 0)),
                pl.BlockSpec((features, features), lambda step, counts: (0, 0)),
            ],
            out_specs=[
                pl.BlockSpec((1, WIN, features), lambda step, counts: (step, 0, 0)),
                pl.BlockSpec((PIECES, PIECE_PAD, LANES), lambda step, counts: (0, 0, 0)),
            ],
            scratch_shapes=[
                pltpu.VMEM((features, 3 * features), jnp.float32),
                pltpu.VMEM((features, features), jnp.float32),
                pltpu.VMEM((1, features), jnp.float32),
            ],
        ),
        out_shape=[
            jax.ShapeDtypeStruct((slots, WIN, features), jnp.bfloat16),
            jax.ShapeDtypeStruct((PIECES, PIECE_PAD, LANES), jnp.bfloat16),
        ],
        compiler_params=pltpu.CompilerParams(
            dimension_semantics=("arbitrary",), vmem_limit_bytes=40 << 20
        ),
        name="window_grads",
    )(own_counts, tokens, d_out, gain, w_qkv, w_out)


def sum_copies(parts, copies, factor):
    def body(in_ref, out_ref):
        total = in_ref[0].astype(jnp.float32)
        for index in range(1, parts.shape[0]):
            total = total + in_ref[index].astype(jnp.float32)
        total = (total * factor).astype(out_ref.dtype)
        for index in range(copies):
            out_ref[index] = total

    return pl.pallas_call(
        body,
        out_shape=jax.ShapeDtypeStruct((copies, *parts.shape[1:]), parts.dtype),
        in_specs=[pl.BlockSpec(memory_space=pltpu.VMEM)],
        out_specs=pl.BlockSpec(memory_space=pltpu.VMEM),
        compiler_params=pltpu.CompilerParams(vmem_limit_bytes=4 << 20),
        name="sum_copies",
    )(parts)


def unpack(whole, features):
    per_column = features // PIECE_ROWS

    def body(in_ref, qkv_ref, out_ref, gain_ref):
        for piece in range(PIECES):
            column, part = divmod(piece, per_column)
            target = qkv_ref if column < 3 * features // LANES else out_ref
            column = column % (3 * features // LANES)
            target[
                part * PIECE_ROWS : (part + 1) * PIECE_ROWS, column * LANES : (column + 1) * LANES
            ] = in_ref[piece, :PIECE_ROWS, :].astype(jnp.float32)
        for piece in range(features // LANES):
            tail = in_ref[piece, PIECE_ROWS:, :].astype(jnp.float32)
            gain_ref[:, piece * LANES : (piece + 1) * LANES] = tail[:1, :]

    return pl.pallas_call(
        body,
        out_shape=[
            jax.ShapeDtypeStruct((features, 3 * features), jnp.float32),
            jax.ShapeDtypeStruct((features, features), jnp.float32),
            jax.ShapeDtypeStruct((1, features), jnp.float32),
        ],
        in_specs=[pl.BlockSpec(memory_space=pltpu.VMEM)],
        out_specs=[pl.BlockSpec(memory_space=pltpu.VMEM)] * 3,
        compiler_params=pltpu.CompilerParams(vmem_limit_bytes=8 << 20),
        name="unpack",
    )(whole)


def in_hbm(array):
    return pltpu.with_memory_space_constraint(array, pltpu.HBM)


def per_device(tokens, d_out, gain, w_qkv, w_out, counts):
    features = tokens.shape[2]
    slot_count = tokens.shape[1] // WIN
    block = ("core", "help", "dp")
    help_index = lax.axis_index("help")
    own_counts = lax.dynamic_slice_in_dim(counts[0], help_index * slot_count, slot_count)
    grad_local, send = local_grads(
        own_counts,
        in_hbm(tokens[0].reshape(slot_count, WIN, features)),
        in_hbm(d_out[0].reshape(slot_count, WIN, features)),
        gain.reshape(1, features),
        w_qkv,
        w_out,
    )
    devices = lax.axis_size("z") * PIECES
    factor = 1.0 / math.sqrt(devices * WKEEP * WIN)
    received = lax.all_to_all(send, block, 0, 0)
    planes = lax.all_to_all(sum_copies(received, lax.axis_size("z"), 1.0), "z", 0, 0)
    whole = lax.all_to_all(sum_copies(planes, PIECES, factor), block, 0, 0)
    grad_qkv, grad_out, grad_gain = unpack(whole, features)
    grad_tokens = grad_local.reshape(1, slot_count * WIN, features)
    return (grad_tokens, grad_qkv, grad_out, grad_gain.reshape(features))


def solution(mesh):
    split = Mesh(
        mesh.devices.reshape(mesh.shape["tile"] // 2, 2, mesh.shape["help"], mesh.shape["dp"]),
        ("z", "core", "help", "dp"),
    )
    tile = ("z", "core")
    in_specs = (
        P("dp", (*tile, "help"), None),
        P("dp", (*tile, "help"), None),
        P(),
        P(),
        P(),
        P("dp", tile),
    )
    out_specs = (P("dp", (*tile, "help"), None), P(), P(), P())
    return jax.shard_map(
        per_device, mesh=split, in_specs=in_specs, out_specs=out_specs, check_vma=False
    )
```

time: 695 us -> 102 us (0.15)
  waiting for transfers between devices: 368 us -> 0 us
  matrix products: 133 us -> 0 us
  local copies, waits for them, and re-layouts: 54.2 us -> 3.3 us
  blocking collectives: 112 us -> 83.3 us
  Pallas kernels: 0 us -> 15.1 us
  between operations: 14.1 us -> 0.66 us
  other arithmetic: 10 us -> 0 us
    psum x1 -> x0, waiting for transfers between devices: 368 us -> none  [per_device(): lax.psum((gain_part, qkv_part, out_part), ('tile', 'help', 'dp'))]
    psum x1 -> x0, blocking collectives: 112 us -> none  [per_device(): lax.psum((gain_part, qkv_part, out_part), ('tile', 'help', 'dp'))]
    dot_general x80 -> x0, matrix products: 103 us -> none  [the longest x8 30 us: window_grads(): jnp.einsum('hqk,qhc->khc', grad_score, query_rows, preferred_element_type...]
    all_to_all x0 -> x3, blocking collectives: none -> 83.3 us  [the longest x1 31.3 us: per_device(): lax.all_to_all(sum_copies(received, lax.axis_size('z'), 1.0), 'z', 0, 0)]
    sub x8 -> x0, matrix products: 30.3 us -> none  [window_grads(): exponent = jnp.exp(scores - highest)]
    slice x32 -> x0, local copies, waits for them, and re-layouts: 25.5 us -> none  [the longest x8 13.2 us: window_grads(): query_rows = projected[:, :features].reshape(-1, HEADS, head_dim)]
    pallas_call x0 -> x4, Pallas kernels: none -> 15.1 us  [the longest x1 13.9 us: local_grads(): pl.pallas_call(kernel, grid_spec=pltpu.PrefetchScalarGridSpec(num_scalar_...]
    dynamic_slice x32 -> x1, local copies, waits for them, and re-layouts: 14.9 us -> 0.07 us  [per_device(): lax.dynamic_slice_in_dim(counts[0], help_index * slot_count, slot_count)]
  transfers between devices with their start and end apart: 1 -> 0, of which waited for: 1 -> 0; matrix products, arithmetic and copies ran while one was open for 0% -> 0% of each run, Pallas kernels for 0% -> 0%
where the time goes in v1:
time: 102 us
  blocking collectives  83.3 us (82%)
  Pallas kernels  15.1 us (15%)
  local copies, waits for them, and re-layouts  3.3 us (3%)
    all_to_all x1, blocking collectives, per_device(): lax.all_to_all(sum_copies(received, lax.axis_size('z'), 1.0), 'z', 0, 0)  31.3 us
    all_to_all x1, blocking collectives, per_device(): received = lax.all_to_all(send, block, 0, 0)  28.5 us
    all_to_all x1, blocking collectives, per_device(): whole = lax.all_to_all(sum_copies(planes, PIECES, factor), block, 0, 0)  23.5 us
    pallas_call x1, Pallas kernels, local_grads(): pl.pallas_call(kernel, grid_spec=pltpu.PrefetchScalarGridSpec(num_scalar_...  13.9 us
    unnamed x8, local copies, waits for them, and re-layouts  3.23 us

profile of v1, /device:TPU:1, one launch (start us, length us, event | category | flops | bytes accessed | tf_op | source)
XLA Modules:
  0.0 102.4 jit_solution(2783337189034317756)
XLA Ops:
  0.6 0.0 copy-start
  0.7 0.6 copy-done
  1.3 0.1 dynamic-slice_bitcast_fusion.counts_ref
  1.4 0.0 copy-start.3
  1.4 0.7 copy-done.3
  2.0 0.0 copy-start.1
  2.0 1.0 copy-done.1
  3.0 0.0 copy-start.2
  3.0 0.9 copy-done.2
  3.9 13.9 %window_grads.1 = (bf16[8,256,256]{2,1,0:T(8,128)(2,1)}, bf16[32,80,128]{2,1,0:T(8,128)(2,1)S(1)}) custom-call(s32[8]{0:T(128)S(1)} %dynamic-slice_bitcast_fusion.counts_ref, bf16[8,256,256]{2,1,0:T(8,128)(2,1)} %bitcast.8, bf16[8,256,256]{2,1,0:T(8,128)(2,1)} %bitcast.9, f32[1,256]{1,0:T(1,128)S(1)} %bitcast.7, bf16[256,768]{1,0:T(8,128)(2,1)S(1)} %copy-done.1, ...), custom_call_target="tpu_custom_call" | custom-call | tf_op jit(solution)/shard_map/window_grads/pallas_call | solution.py:164
  17.9 28.5 %all_to_all.15.in_ref = bf16[32,80,128]{2,1,0:T(8,128)(2,1)S(1)} all-to-all(bf16[32,80,128]{2,1,0:T(8,128)(2,1)S(1)} %get-tuple-element.10), channel_id=1, replica_groups=mesh['z'=16,'core'=2,'help'=4,'dp'=4] {'core','help','dp'}, dimensions={0} | all-to-all | bytes 1310720 | tf_op jit(solution)/shard_map/all_to_all | solution.py:265
  46.4 0.1 sum_copies.2
  46.5 31.3 %all_to_all.16.in_ref = bf16[16,80,128]{2,1,0:T(8,128)(2,1)S(1)} all-to-all(bf16[16,80,128]{2,1,0:T(8,128)(2,1)S(1)} %sum_copies.2), channel_id=1, replica_groups=mesh['z'=16,'core'=2,'help'=4,'dp'=4] {'z'}, dimensions={0} | all-to-all | bytes 655360 | tf_op jit(solution)/shard_map/all_to_all | solution.py:266
  77.8 0.1 sum_copies.3
  77.9 23.5 %all_to_all.17.in_ref = bf16[32,80,128]{2,1,0:T(8,128)(2,1)S(1)} all-to-all(bf16[32,80,128]{2,1,0:T(8,128)(2,1)S(1)} %sum_copies.3), channel_id=1, replica_groups=mesh['z'=16,'core'=2,'help'=4,'dp'=4] {'core','help','dp'}, dimensions={0} | all-to-all | bytes 1310720 | tf_op jit(solution)/shard_map/all_to_all | solution.py:267
  101.4 1.0 unpack.1
Async XLA Ops:
  0.6 0.7 copy-start
  1.4 0.7 copy-start.3
  2.0 1.0 copy-start.1
  3.0 0.9 copy-start.2

commit v2 on v1

v2 whole, which is shorter than its diff:
```python
import functools
import math

import jax
import jax.numpy as jnp
from jax import lax
from jax.experimental import pallas as pl
from jax.experimental.pallas import tpu as pltpu
from jax.sharding import Mesh
from jax.sharding import PartitionSpec as P

HEADS = 8
WIN = 256
WKEEP = 6
LANES = 128
ROW_STEP = 64
PIECES = 64
PIECE_ROWS = 32


def dot_nn(a, b):
    return jnp.dot(a, b, preferred_element_type=jnp.float32)


def dot_nt(a, b):
    return lax.dot_general(a, b, (((1,), (1,)), ((), ())), preferred_element_type=jnp.float32)


def window_rows(rows, count, x_ref, u_ref, gain, wqkv_ref, wout_ref, qkv_ref, out_ref, g_ref):
    features = x_ref.shape[-1]
    head_dim = features // HEADS
    per_tile = LANES // head_dim
    factor = 1.0 / math.sqrt(head_dim)
    log_factor = factor * math.log2(math.e)
    half = jnp.bfloat16
    active = lax.broadcasted_iota(jnp.int32, (rows, 1), 0) < count
    tokens = jnp.where(active, x_ref[0, :rows, :].astype(jnp.float32), 0.0)
    upstream = jnp.where(active, u_ref[0, :rows, :].astype(jnp.float32), 0.0)
    upstream_half = upstream.astype(half)
    center = tokens - jnp.mean(tokens, axis=-1, keepdims=True)
    inverse = lax.rsqrt(jnp.mean(center * center, axis=-1, keepdims=True) + 1e-05)
    normed = center * inverse
    hidden = (normed * gain).astype(half)
    queries = dot_nn(hidden, wqkv_ref[:, :features]).astype(half)
    keys = dot_nn(hidden, wqkv_ref[:, features : 2 * features]).astype(half)
    values = dot_nn(hidden, wqkv_ref[:, 2 * features :]).astype(half)
    grad_attn = dot_nt(upstream_half, wout_ref[...]).astype(half)
    hidden_t = hidden.T
    keys_t = keys.T
    values_t = values.T
    lane = lax.broadcasted_iota(jnp.int32, (rows, LANES), 1) // head_dim
    zero = jnp.zeros((), half)

    def masked(array, head):
        tile, place = divmod(head, per_tile)
        block = array[:, tile * LANES : (tile + 1) * LANES]
        return jnp.where(lane == place, block, zero)

    def tile_of(array, head):
        tile = head // per_tile
        return array[:, tile * LANES : (tile + 1) * LANES]

    def products(head):
        scores = dot_nt(masked(keys, head), tile_of(queries, head))
        grad_prob = dot_nt(masked(values, head), tile_of(grad_attn, head))
        return scores, grad_prob

    def gathered(lefts, array, group):
        right = jnp.concatenate([masked(array, head) for head in group], axis=0)
        return dot_nn(jnp.concatenate(lefts, axis=1), right).astype(half)

    attended_parts, query_parts = [], []
    key_tiles, value_tiles = [], []
    probs, scored = [], []
    ready = products(0)
    for head in range(HEADS):
        scores, grad_prob = ready
        if head + 1 < HEADS:
            ready = products(head + 1)
        last = jnp.where(active[-ROW_STEP:], scores[-ROW_STEP:], -1e30)
        scores = jnp.concatenate([scores[:-ROW_STEP], last], axis=0) if rows > ROW_STEP else last
        highest = jnp.max(scores, axis=0, keepdims=True)
        exponent = jnp.exp2((scores - highest) * log_factor)
        probability = exponent * (1.0 / jnp.sum(exponent, axis=0, keepdims=True))
        prob_half = probability.astype(half)
        row_sum = jnp.sum(probability * grad_prob, axis=0, keepdims=True)
        grad_score = (probability * (grad_prob - row_sum) * factor).astype(half)
        span = slice(head * head_dim, (head + 1) * head_dim)
        attended_parts.append(dot_nn(values_t[span, :], prob_half).astype(half))
        query_parts.append(dot_nn(keys_t[span, :], grad_score).astype(half))
        probs.append(prob_half)
        scored.append(grad_score)
        if len(probs) == per_tile:
            group = range(head + 1 - per_tile, head + 1)
            value_tiles.append(gathered(probs, grad_attn, group))
            key_tiles.append(gathered(scored, queries, group))
            probs, scored = [], []
    attended_t = jnp.concatenate(attended_parts, axis=0)
    grad_query = jnp.concatenate(query_parts, axis=0).T
    grad_key = jnp.concatenate(key_tiles, axis=1)
    grad_value = jnp.concatenate(value_tiles, axis=1)
    grad_proj = jnp.concatenate([grad_query, grad_key, grad_value], axis=1)
    grad_hidden = dot_nt(grad_proj, wqkv_ref[...])
    qkv_ref[...] += dot_nn(hidden_t, grad_proj)
    out_ref[...] += dot_nn(attended_t, upstream_half)
    grad_norm = grad_hidden * gain
    mean_one = jnp.mean(grad_norm, axis=-1, keepdims=True)
    mean_two = jnp.mean(grad_norm * normed, axis=-1, keepdims=True)
    grad_input = inverse * (grad_norm - mean_one - normed * mean_two)
    g_ref[0, :rows, :] = jnp.where(active, upstream + grad_input, 0.0).astype(half)
    if rows < WIN:
        g_ref[0, rows:, :] = jnp.zeros((WIN - rows, features), half)


def kernel(counts_ref, x_ref, u_ref, gain_ref, wqkv_ref, wout_ref, g_ref, send_ref, qkv_ref, out_ref):
    step = pl.program_id(0)
    features = x_ref.shape[-1]

    @pl.when(step == 0)
    def _():
        qkv_ref[...] = jnp.zeros_like(qkv_ref)
        out_ref[...] = jnp.zeros_like(out_ref)

    count = counts_ref[0, lax.axis_index("help") * pl.num_programs(0) + step]

    @pl.when(count == 0)
    def _():
        g_ref[...] = jnp.zeros_like(g_ref)

    for rows in range(ROW_STEP, WIN + 1, ROW_STEP):
        @pl.when(jnp.logical_and(count > rows - ROW_STEP, count <= rows))
        def _(rows=rows):
            window_rows(rows, count, x_ref, u_ref, gain_ref[...], wqkv_ref, wout_ref, qkv_ref, out_ref, g_ref)

    @pl.when(step == pl.num_programs(0) - 1)
    def _():
        for piece in range(PIECES):
            source, rows, lanes = place_of(piece, features, qkv_ref, out_ref)
            send_ref[piece] = source[rows, lanes].astype(send_ref.dtype)


def place_of(piece, features, qkv_ref, out_ref):
    column, part = divmod(piece, features // PIECE_ROWS)
    columns = 3 * features // LANES
    lane = column % columns * LANES
    rows = slice(part * PIECE_ROWS, (part + 1) * PIECE_ROWS)
    return (qkv_ref if column < columns else out_ref), rows, slice(lane, lane + LANES)


def local_grads(counts, tokens, d_out, gain, w_qkv, w_out):
    slots, features = tokens.shape[0], gain.shape[-1]
    return pl.pallas_call(
        kernel,
        grid_spec=pltpu.PrefetchScalarGridSpec(
            num_scalar_prefetch=1,
            grid=(slots,),
            in_specs=[
                pl.BlockSpec((1, WIN, features), lambda step, counts: (step, 0, 0)),
                pl.BlockSpec((1, WIN, features), lambda step, counts: (step, 0, 0)),
                pl.BlockSpec((1, features), lambda step, counts: (0, 0)),
                pl.BlockSpec((features, 3 * features), lambda step, counts: (0, 0)),
                pl.BlockSpec((features, features), lambda step, counts: (0, 0)),
            ],
            out_specs=[
                pl.BlockSpec((1, WIN, features), lambda step, counts: (step, 0, 0)),
                pl.BlockSpec((PIECES, PIECE_ROWS, LANES), lambda step, counts: (0, 0, 0)),
            ],
            scratch_shapes=[
                pltpu.VMEM((features, 3 * features), jnp.float32),
                pltpu.VMEM((features, features), jnp.float32),
            ],
        ),
        out_shape=[
            jax.ShapeDtypeStruct((slots, WIN, features), jnp.bfloat16),
            jax.ShapeDtypeStruct((PIECES, PIECE_ROWS, LANES), jnp.bfloat16),
        ],
        compiler_params=pltpu.CompilerParams(
            dimension_semantics=("arbitrary",), vmem_limit_bytes=40 << 20
        ),
        name="window_grads",
    )(counts, tokens, d_out, gain, w_qkv, w_out)


def sum_copies(parts, copies, factor, dtype):
    def body(in_ref, out_ref):
        total = in_ref[0].astype(jnp.float32)
        for index in range(1, parts.shape[0]):
            total = total + in_ref[index].astype(jnp.float32)
        total = (total * factor).astype(dtype)
        for index in range(copies):
            out_ref[index] = total

    return pl.pallas_call(
        body,
        out_shape=jax.ShapeDtypeStruct((copies, *parts.shape[1:]), dtype),
        in_specs=[pl.BlockSpec(memory_space=pltpu.VMEM)],
        out_specs=pl.BlockSpec(memory_space=pltpu.VMEM),
        compiler_params=pltpu.CompilerParams(vmem_limit_bytes=4 << 20),
        name="sum_copies",
    )(parts)


def unpack(whole, w_qkv, gain):
    features = gain.shape[-1]

    def body(in_ref, w_ref, scale_ref, qkv_ref, out_ref, gain_ref):
        for piece in range(PIECES):
            target, rows, lanes = place_of(piece, features, qkv_ref, out_ref)
            target[rows, lanes] = in_ref[piece].astype(jnp.float32)
        total = jnp.zeros((features, LANES), jnp.float32)
        for lane in range(0, 3 * features, LANES):
            lanes = slice(lane, lane + LANES)
            total = total + w_ref[:, lanes].astype(jnp.float32) * qkv_ref[:, lanes]
        gain_ref[...] = jnp.sum(total.T, axis=0, keepdims=True) / scale_ref[...]

    return pl.pallas_call(
        body,
        out_shape=[
            jax.ShapeDtypeStruct((features, 3 * features), jnp.float32),
            jax.ShapeDtypeStruct((features, features), jnp.float32),
            jax.ShapeDtypeStruct((1, features), jnp.float32),
        ],
        in_specs=[pl.BlockSpec(memory_space=pltpu.VMEM)] * 3,
        out_specs=[pl.BlockSpec(memory_space=pltpu.VMEM)] * 3,
        compiler_params=pltpu.CompilerParams(vmem_limit_bytes=8 << 20),
        name="unpack",
    )(whole, w_qkv, gain)


def in_hbm(array):
    return pltpu.with_memory_space_constraint(array, pltpu.HBM)


def per_device(tokens, d_out, gain, w_qkv, w_out, counts):
    features = tokens.shape[2]
    slot_count = tokens.shape[1] // WIN
    block = ("z_lo", "core", "help", "dp")
    gain = gain.reshape(1, features)
    grad_local, send = local_grads(
        counts,
        in_hbm(tokens[0].reshape(slot_count, WIN, features)),
        in_hbm(d_out[0].reshape(slot_count, WIN, features)),
        in_hbm(gain),
        in_hbm(w_qkv),
        in_hbm(w_out),
    )
    planes = lax.axis_size("z_hi")
    factor = 1.0 / math.sqrt(planes * lax.axis_size(block) * WKEEP * WIN)
    received = lax.all_to_all(send, block, 0, 0)
    copies = sum_copies(received, planes, 1.0, jnp.float32)
    copies = sum_copies(lax.all_to_all(copies, "z_hi", 0, 0), PIECES, factor, jnp.bfloat16)
    grad_qkv, grad_out, grad_gain = unpack(lax.all_to_all(copies, block, 0, 0), w_qkv, gain)
    grad_tokens = grad_local.reshape(1, slot_count * WIN, features)
    return (grad_tokens, grad_qkv, grad_out, grad_gain.reshape(features))


def solution(mesh):
    shape = dict(mesh.shape)
    split = Mesh(
        mesh.devices.reshape(shape["tile"] // 4, 2, 2, shape["help"], shape["dp"]),
        ("z_hi", "z_lo", "core", "help", "dp"),
    )
    tile = ("z_hi", "z_lo", "core")
    in_specs = (
        P("dp", (*tile, "help"), None),
        P("dp", (*tile, "help"), None),
        P(),
        P(),
        P(),
        P("dp", tile),
    )
    out_specs = (P("dp", (*tile, "help"), None), P(), P(), P())
    return jax.shard_map(
        per_device, mesh=split, in_specs=in_specs, out_specs=out_specs, check_vma=False
    )
```

time: 102 us -> 93.8 us (0.920); the launches traced: 102 us -> 92.8 us
  blocking collectives: 83.3 us -> 69.7 us
  Pallas kernels: 15.1 us -> 21.8 us
  local copies, waits for them, and re-layouts: 3.3 us -> 0.66 us
    all_to_all x2, blocking collectives: 54.8 us -> 45.4 us  [the longest x1 26 us: per_device(): lax.all_to_all(copies, 'z_hi', 0, 0)]
    pallas_call x1, Pallas kernels: 13.9 us -> 20.6 us  [local_grads(): pl.pallas_call(kernel, grid_spec=pltpu.PrefetchScalarGridSpec(num_scalar_...]
    all_to_all x1, blocking collectives: 28.5 us -> 24.2 us  [per_device(): received = lax.all_to_all(send, block, 0, 0)]
    unnamed x8 -> x6, local copies, waits for them, and re-layouts: 3.23 us -> 0.66 us
where the time goes in v2:
time: 93.8 us; the launch traced here: 92.8 us
  blocking collectives  69.7 us (74%)
  Pallas kernels  21.8 us (23%)
    all_to_all x1, blocking collectives, per_device(): lax.all_to_all(copies, 'z_hi', 0, 0)  26 us
    all_to_all x1, blocking collectives, per_device(): received = lax.all_to_all(send, block, 0, 0)  24.2 us
    pallas_call x1, Pallas kernels, local_grads(): pl.pallas_call(kernel, grid_spec=pltpu.PrefetchScalarGridSpec(num_scalar_...  20.6 us
    all_to_all x1, blocking collectives, per_device(): lax.all_to_all(copies, block, 0, 0)  19.4 us

profile of v2, /device:TPU:1, one launch (start us, length us, event | category | flops | bytes accessed | tf_op | source)
XLA Modules:
  0.0 92.8 jit_solution(6321526338316876743)
XLA Ops:
  0.6 0.0 copy-start.2
  0.6 0.6 copy-done.2
  1.3 20.6 %window_grads.1 = (bf16[8,256,256]{2,1,0:T(8,128)(2,1)}, bf16[64,32,128]{2,1,0:T(8,128)(2,1)S(1)}) custom-call(s32[1,32]{1,0:T(1,128)S(1)} %copy-done.2, bf16[8,256,256]{2,1,0:T(8,128)(2,1)} %bitcast.7, bf16[8,256,256]{2,1,0:T(8,128)(2,1)} %bitcast.8, f32[1,256]{1,0:T(1,128)} %bitcast.5, bf16[256,768]{1,0:T(8,128)(2,1)} %w_ref.1, bf16[256,256]{1,0:T(8,128)(2,1)} %wout_ref.1), custom_call_target="tpu_custom_call" | custom-call | tf_op jit(solution)/shard_map/window_grads/pallas_call | solution.py:152
  21.9 24.2 %all_to_all.15.in_ref = bf16[64,32,128]{2,1,0:T(8,128)(2,1)S(1)} all-to-all(bf16[64,32,128]{2,1,0:T(8,128)(2,1)S(1)} %get-tuple-element.10), channel_id=1, replica_groups=mesh['z_hi'=8,'z_lo'=2,'core'=2,'help'=4,'dp'=4] {'z_lo','core','help','..., dimensions={0} | all-to-all | bytes 1048576 | tf_op jit(solution)/shard_map/all_to_all | solution.py:249
  46.2 0.1 sum_copies.2
  46.3 26.0 %all_to_all.16.in_ref = f32[8,32,128]{2,1,0:T(8,128)S(1)} all-to-all(f32[8,32,128]{2,1,0:T(8,128)S(1)} %sum_copies.2), channel_id=1, replica_groups=mesh['z_hi'=8,'z_lo'=2,'core'=2,'help'=4,'dp'=4] {'z_hi'}, dimensions={0} | all-to-all | bytes 262144 | tf_op jit(solution)/shard_map/all_to_all | solution.py:251
  72.4 0.0 copy-start
  72.4 0.0 copy-start.1
  72.4 19.4 %all_to_all.17.in_ref = bf16[64,32,128]{2,1,0:T(8,128)(2,1)S(1)} all-to-all(bf16[64,32,128]{2,1,0:T(8,128)(2,1)S(1)} %sum_copies.3), channel_id=1, replica_groups=mesh['z_hi'=8,'z_lo'=2,'core'=2,'help'=4,'dp'=4] {'z_lo','core','help','..., dimensions={0} | all-to-all | bytes 1048576 | tf_op jit(solution)/shard_map/all_to_all | solution.py:252
  91.8 0.0 copy-done
  91.8 0.0 copy-done.1
  91.8 1.1 %unpack.1 = (f32[256,768]{1,0:T(8,128)}, f32[256,256]{1,0:T(8,128)}, f32[1,256]{1,0:T(1,128)}) custom-call(bf16[64,32,128]{2,1,0:T(8,128)(2,1)S(1)} %all_to_all.17.in_ref, bf16[256,768]{1,0:T(8,128)(2,1)S(1)} %copy-done, f32[1,256]{1,0:T(1,128)S(1)} %bitcast.6), custom_call_target="tpu_custom_call" | custom-call | tf_op jit(solution)/shard_map/unpack/pallas_call | solution.py:216
  (1 shorter events, 0.0 us)
Async XLA Ops:
  0.6 0.7 copy-start.2
  72.4 19.4 %copy-start = (bf16[256,768]{1,0:T(8,128)(2,1)S(1)}, bf16[256,768]{1,0:T(8,128)(2,1)}, u32[]{:S(2)}) copy-start(bf16[256,768]{1,0:T(8,128)(2,1)} %w_ref.1) | copy-start | bytes 1179652
  72.4 19.4 %copy-start.1 = (f32[256]{0:T(256)S(1)}, f32[256]{0:T(256)}, u32[]{:S(2)}) copy-start(f32[256]{0:T(256)} %param.8) | copy-start | bytes 3076

commit v3 on v2

v3 whole, which is shorter than its diff:
```python
import functools
import math

import jax
import jax.numpy as jnp
from jax import lax
from jax.experimental import pallas as pl
from jax.experimental.pallas import tpu as pltpu
from jax.sharding import Mesh
from jax.sharding import PartitionSpec as P

HEADS = 8
WIN = 256
WKEEP = 6
LANES = 128
ROW_STEP = 64
PER_STEP = 2
GROUPS = {64: 8, 128: 4, 192: 1, 256: 2}
PIECES = 64
PIECE_ROWS = 32


def dot_nn(a, b):
    return jnp.dot(a, b, preferred_element_type=jnp.float32)


def dot_nt(a, b):
    return lax.dot_general(a, b, (((1,), (1,)), ((), ())), preferred_element_type=jnp.float32)


def window_rows(rows, place, count, x_ref, u_ref, gain, wqkv_ref, wqkv_t_ref, wout_t_ref, sum_ref, g_ref):
    features = x_ref.shape[-1]
    head_dim = features // HEADS
    factor = 1.0 / math.sqrt(head_dim)
    log_factor = factor * math.log2(math.e)
    half = jnp.bfloat16
    active = lax.broadcasted_iota(jnp.int32, (rows, 1), 0) < count
    tokens = jnp.where(active, x_ref[place, :rows, :].astype(jnp.float32), 0.0)
    upstream = jnp.where(active, u_ref[place, :rows, :].astype(jnp.float32), 0.0)
    upstream_half = upstream.astype(half)
    grad_attn_t = dot_nn(upstream_half, wout_t_ref[...]).astype(half).T
    center = tokens - jnp.mean(tokens, axis=-1, keepdims=True)
    inverse = lax.rsqrt(jnp.mean(center * center, axis=-1, keepdims=True) + 1e-05)
    normed = center * inverse
    hidden = (normed * gain).astype(half)
    queries_t = dot_nn(hidden, wqkv_ref[:, :features]).astype(half).T
    keys = dot_nn(hidden, wqkv_ref[:, features : 2 * features]).astype(half)
    values = dot_nn(hidden, wqkv_ref[:, 2 * features :]).astype(half)
    keys_t = keys.T
    values_t = values.T

    def span(head):
        return slice(head * head_dim, (head + 1) * head_dim)

    size = GROUPS[rows]

    def products(start):
        heads = range(start, start + size)
        scores = [dot_nn(keys[:, span(head)], queries_t[span(head), :]) for head in heads]
        grad_prob = [dot_nn(values[:, span(head)], grad_attn_t[span(head), :]) for head in heads]
        return jnp.concatenate(scores, axis=1), jnp.concatenate(grad_prob, axis=1)

    attended, grad_query, grad_key, grad_value = [], [], [], []
    ready = products(0)
    for start in range(0, HEADS, size):
        scores, grad_prob = ready
        if start + size < HEADS:
            ready = products(start + size)
        last = jnp.where(active[-ROW_STEP:], scores[-ROW_STEP:], -1e30)
        scores = jnp.concatenate([scores[:-ROW_STEP], last], axis=0) if rows > ROW_STEP else last
        highest = jnp.max(scores, axis=0, keepdims=True)
        exponent = jnp.exp2((scores - highest) * log_factor)
        probability = exponent * (1.0 / jnp.sum(exponent, axis=0, keepdims=True))
        prob_group = probability.astype(half)
        row_sum = jnp.sum(probability * grad_prob, axis=0, keepdims=True)
        score_group = (probability * (grad_prob - row_sum) * factor).astype(half)
        for index in range(size):
            head = start + index
            prob_half = prob_group[:, index * rows : (index + 1) * rows]
            grad_score = score_group[:, index * rows : (index + 1) * rows]
            attended.append(dot_nn(values_t[span(head), :], prob_half).astype(half))
            grad_value.append(dot_nt(grad_attn_t[span(head), :], prob_half).astype(half))
            grad_query.append(dot_nn(keys_t[span(head), :], grad_score).astype(half))
            grad_key.append(dot_nt(queries_t[span(head), :], grad_score).astype(half))
    grad_proj_t = jnp.concatenate([*grad_query, *grad_key, *grad_value], axis=0)
    grad_hidden = dot_nn(grad_proj_t.T, wqkv_t_ref[...])
    sum_ref[: 3 * features, :] += dot_nn(grad_proj_t, hidden)
    sum_ref[3 * features :, :] += dot_nn(jnp.concatenate(attended, axis=0), upstream_half)
    grad_norm = grad_hidden * gain
    mean_one = jnp.mean(grad_norm, axis=-1, keepdims=True)
    mean_two = jnp.mean(grad_norm * normed, axis=-1, keepdims=True)
    grad_input = inverse * (grad_norm - mean_one - normed * mean_two)
    g_ref[place, :rows, :] = jnp.where(active, upstream + grad_input, 0.0).astype(half)
    if rows < WIN:
        g_ref[place, rows:, :] = jnp.zeros((WIN - rows, features), half)


def kernel(counts_ref, x_ref, u_ref, gain_ref, wqkv_ref, wout_ref, g_ref, send_ref, sum_ref, wqkv_t_ref, wout_t_ref):
    step = pl.program_id(0)

    @pl.when(step == 0)
    def _():
        sum_ref[...] = jnp.zeros_like(sum_ref)
        wout_t_ref[...] = wout_ref[...].T
        wqkv_t_ref[...] = wqkv_ref[...].T

    slots = pl.num_programs(0) * PER_STEP
    first = lax.axis_index("help") * slots + step * PER_STEP

    def window_step(place, carry):
        count = counts_ref[0, first + place]

        @pl.when(count == 0)
        def _():
            g_ref[place] = jnp.zeros(g_ref.shape[1:], g_ref.dtype)

        for rows in range(ROW_STEP, WIN + 1, ROW_STEP):
            @pl.when(jnp.logical_and(count > rows - ROW_STEP, count <= rows))
            def _(rows=rows):
                window_rows(
                    rows,
                    place,
                    count,
                    x_ref,
                    u_ref,
                    gain_ref[...],
                    wqkv_ref,
                    wqkv_t_ref,
                    wout_t_ref,
                    sum_ref,
                    g_ref,
                )

        return carry

    lax.fori_loop(0, PER_STEP, window_step, 0)

    @pl.when(step == pl.num_programs(0) - 1)
    def _():
        for piece in range(PIECES):
            rows, lanes = place_of(piece)
            send_ref[piece] = sum_ref[rows, lanes].astype(send_ref.dtype)


def place_of(piece):
    part, lane = divmod(piece, WIN // LANES)
    return slice(part * PIECE_ROWS, (part + 1) * PIECE_ROWS), slice(lane * LANES, (lane + 1) * LANES)


def local_grads(counts, tokens, d_out, gain, w_qkv, w_out):
    slots, features = tokens.shape[0], gain.shape[-1]
    return pl.pallas_call(
        kernel,
        grid_spec=pltpu.PrefetchScalarGridSpec(
            num_scalar_prefetch=1,
            grid=(slots // PER_STEP,),
            in_specs=[
                pl.BlockSpec((PER_STEP, WIN, features), lambda step, counts: (step, 0, 0)),
                pl.BlockSpec((PER_STEP, WIN, features), lambda step, counts: (step, 0, 0)),
                pl.BlockSpec((1, features), lambda step, counts: (0, 0)),
                pl.BlockSpec((features, 3 * features), lambda step, counts: (0, 0)),
                pl.BlockSpec((features, features), lambda step, counts: (0, 0)),
            ],
            out_specs=[
                pl.BlockSpec((PER_STEP, WIN, features), lambda step, counts: (step, 0, 0)),
                pl.BlockSpec(memory_space=pltpu.VMEM),
            ],
            scratch_shapes=[
                pltpu.VMEM((4 * features, features), jnp.float32),
                pltpu.VMEM((3 * features, features), jnp.bfloat16),
                pltpu.VMEM((features, features), jnp.bfloat16),
            ],
        ),
        out_shape=[
            jax.ShapeDtypeStruct((slots, WIN, features), jnp.bfloat16),
            jax.ShapeDtypeStruct((PIECES, PIECE_ROWS, LANES), jnp.bfloat16),
        ],
        compiler_params=pltpu.CompilerParams(
            dimension_semantics=("arbitrary",), vmem_limit_bytes=40 << 20
        ),
        name="window_grads",
    )(counts, tokens, d_out, gain, w_qkv, w_out)


def sum_copies(parts, copies, factor, dtype):
    def body(in_ref, out_ref):
        total = in_ref[0].astype(jnp.float32)
        for index in range(1, parts.shape[0]):
            total = total + in_ref[index].astype(jnp.float32)
        total = (total * factor).astype(dtype)
        for index in range(copies):
            out_ref[index] = total

    return pl.pallas_call(
        body,
        out_shape=jax.ShapeDtypeStruct((copies, *parts.shape[1:]), dtype),
        in_specs=[pl.BlockSpec(memory_space=pltpu.VMEM)],
        out_specs=pl.BlockSpec(memory_space=pltpu.VMEM),
        compiler_params=pltpu.CompilerParams(vmem_limit_bytes=4 << 20),
        name="sum_copies",
    )(parts)


def unpack(whole, w_qkv, gain):
    features = gain.shape[-1]

    def body(in_ref, w_ref, scale_ref, qkv_ref, out_ref, gain_ref, turned_ref):
        for piece in range(PIECES):
            rows, lanes = place_of(piece)
            if rows.start < 3 * features:
                turned_ref[rows, lanes] = in_ref[piece]
            else:
                out_ref[rows.start - 3 * features : rows.stop - 3 * features, lanes] = in_ref[piece].astype(jnp.float32)
        for block in range(3):
            columns = slice(block * features, (block + 1) * features)
            qkv_ref[:, columns] = turned_ref[columns, :].T.astype(jnp.float32)
        total = jnp.zeros((features, LANES), jnp.float32)
        for lane in range(0, 3 * features, LANES):
            lanes = slice(lane, lane + LANES)
            total = total + w_ref[:, lanes].astype(jnp.float32) * qkv_ref[:, lanes]
        gain_ref[...] = jnp.sum(total.T, axis=0, keepdims=True) / scale_ref[...]

    return pl.pallas_call(
        body,
        out_shape=[
            jax.ShapeDtypeStruct((features, 3 * features), jnp.float32),
            jax.ShapeDtypeStruct((features, features), jnp.float32),
            jax.ShapeDtypeStruct((1, features), jnp.float32),
        ],
        in_specs=[pl.BlockSpec(memory_space=pltpu.VMEM)] * 3,
        out_specs=[pl.BlockSpec(memory_space=pltpu.VMEM)] * 3,
        scratch_shapes=[pltpu.VMEM((3 * features, features), jnp.bfloat16)],
        compiler_params=pltpu.CompilerParams(vmem_limit_bytes=8 << 20),
        name="unpack",
    )(whole, w_qkv, gain)


def in_hbm(array):
    return pltpu.with_memory_space_constraint(array, pltpu.HBM)


def per_device(tokens, d_out, gain, w_qkv, w_out, counts):
    features = tokens.shape[2]
    slot_count = tokens.shape[1] // WIN
    block = ("z_lo", "core", "help", "dp")
    gain = gain.reshape(1, features)
    grad_local, send = local_grads(
        in_hbm(counts),
        in_hbm(tokens[0].reshape(slot_count, WIN, features)),
        in_hbm(d_out[0].reshape(slot_count, WIN, features)),
        in_hbm(gain),
        in_hbm(w_qkv),
        in_hbm(w_out),
    )
    planes = lax.axis_size("z_hi")
    factor = 1.0 / math.sqrt(planes * lax.axis_size(block) * WKEEP * WIN)
    received = lax.all_to_all(send, block, 0, 0)
    copies = sum_copies(received, planes, 1.0, jnp.float32)
    copies = sum_copies(lax.all_to_all(copies, "z_hi", 0, 0), PIECES, factor, jnp.bfloat16)
    grad_qkv, grad_out, grad_gain = unpack(lax.all_to_all(copies, block, 0, 0), w_qkv, gain)
    grad_tokens = grad_local.reshape(1, slot_count * WIN, features)
    return (grad_tokens, grad_qkv, grad_out, grad_gain.reshape(features))


def solution(mesh):
    shape = dict(mesh.shape)
    split = Mesh(
        mesh.devices.reshape(shape["tile"] // 4, 2, 2, shape["help"], shape["dp"]),
        ("z_hi", "z_lo", "core", "help", "dp"),
    )
    tile = ("z_hi", "z_lo", "core")
    in_specs = (
        P("dp", (*tile, "help"), None),
        P("dp", (*tile, "help"), None),
        P(),
        P(),
        P(),
        P("dp", tile),
    )
    out_specs = (P("dp", (*tile, "help"), None), P(), P(), P())
    return jax.shard_map(
        per_device, mesh=split, in_specs=in_specs, out_specs=out_specs, check_vma=False
    )
```

time: 93.8 us -> 91.8 us (0.979)
  Pallas kernels: 21.8 us -> 12.4 us
  blocking collectives: 69.7 us -> 78.5 us
    pallas_call x1, Pallas kernels: 20.6 us -> 11.1 us  [local_grads(): pl.pallas_call(kernel, grid_spec=pltpu.PrefetchScalarGridSpec(num_scalar_...]
    all_to_all x1, blocking collectives: 24.2 us -> 30.4 us  [per_device(): received = lax.all_to_all(send, block, 0, 0)]
    all_to_all x1, blocking collectives: 26 us -> 28.7 us  [per_device(): lax.all_to_all(copies, 'z_hi', 0, 0)]
where the time goes in v3:
time: 91.8 us; the launch traced here: 91.6 us
  blocking collectives  78.5 us (86%)
  Pallas kernels  12.4 us (14%)
    all_to_all x1, blocking collectives, per_device(): received = lax.all_to_all(send, block, 0, 0)  30.4 us
    all_to_all x1, blocking collectives, per_device(): lax.all_to_all(copies, 'z_hi', 0, 0)  28.7 us
    all_to_all x1, blocking collectives, per_device(): lax.all_to_all(copies, block, 0, 0)  19.4 us
    pallas_call x1, Pallas kernels, local_grads(): pl.pallas_call(kernel, grid_spec=pltpu.PrefetchScalarGridSpec(num_scalar_...  11.1 us

profile of v3, /device:TPU:1, one launch (start us, length us, event | category | flops | bytes accessed | tf_op | source)
XLA Modules:
  0.0 91.6 jit_solution(6012243694126715233)
XLA Ops:
  0.6 11.1 %window_grads.1 = (bf16[8,256,256]{2,1,0:T(8,128)(2,1)}, bf16[64,32,128]{2,1,0:T(8,128)(2,1)S(1)}) custom-call(s32[1,32]{1,0:T(1,128)} %counts_ref.1, bf16[8,256,256]{2,1,0:T(8,128)(2,1)} %bitcast.7, bf16[8,256,256]{2,1,0:T(8,128)(2,1)} %bitcast.8, f32[1,256]{1,0:T(1,128)} %bitcast.5, bf16[256,768]{1,0:T(8,128)(2,1)} %w_ref.1, bf16[256,256]{1,0:T(8,128)(2,1)} %wout_ref.1), custom_call_target="tpu_custom_call" | custom-call | tf_op jit(solution)/shard_map/window_grads/pallas_call | solution.py:152
  11.8 30.4 %all_to_all.15.in_ref = bf16[64,32,128]{2,1,0:T(8,128)(2,1)S(1)} all-to-all(bf16[64,32,128]{2,1,0:T(8,128)(2,1)S(1)} %get-tuple-element.10), channel_id=1, replica_groups=mesh['z_hi'=8,'z_lo'=2,'core'=2,'help'=4,'dp'=4] {'z_lo','core','help','..., dimensions={0} | all-to-all | bytes 1048576 | tf_op jit(solution)/shard_map/all_to_all | solution.py:257
  42.2 0.1 sum_copies.2
  42.3 28.7 %all_to_all.16.in_ref = f32[8,32,128]{2,1,0:T(8,128)S(1)} all-to-all(f32[8,32,128]{2,1,0:T(8,128)S(1)} %sum_copies.2), channel_id=1, replica_groups=mesh['z_hi'=8,'z_lo'=2,'core'=2,'help'=4,'dp'=4] {'z_hi'}, dimensions={0} | all-to-all | bytes 262144 | tf_op jit(solution)/shard_map/all_to_all | solution.py:259
  71.0 0.0 copy-start
  71.0 0.0 copy-start.1
  71.0 19.4 %all_to_all.17.in_ref = bf16[64,32,128]{2,1,0:T(8,128)(2,1)S(1)} all-to-all(bf16[64,32,128]{2,1,0:T(8,128)(2,1)S(1)} %sum_copies.3), channel_id=1, replica_groups=mesh['z_hi'=8,'z_lo'=2,'core'=2,'help'=4,'dp'=4] {'z_lo','core','help','..., dimensions={0} | all-to-all | bytes 1048576 | tf_op jit(solution)/shard_map/all_to_all | solution.py:260
  90.4 0.0 copy-done
  90.4 0.0 copy-done.1
  90.4 1.1 %unpack.1 = (f32[256,768]{1,0:T(8,128)}, f32[256,256]{1,0:T(8,128)}, f32[1,256]{1,0:T(1,128)}) custom-call(bf16[64,32,128]{2,1,0:T(8,128)(2,1)S(1)} %all_to_all.17.in_ref, bf16[256,768]{1,0:T(8,128)(2,1)S(1)} %copy-done, f32[1,256]{1,0:T(1,128)S(1)} %bitcast.6), custom_call_target="tpu_custom_call" | custom-call | tf_op jit(solution)/shard_map/unpack/pallas_call | solution.py:223
  (1 shorter events, 0.0 us)
Async XLA Ops:
  71.0 19.4 %copy-start = (bf16[256,768]{1,0:T(8,128)(2,1)S(1)}, bf16[256,768]{1,0:T(8,128)(2,1)}, u32[]{:S(2)}) copy-start(bf16[256,768]{1,0:T(8,128)(2,1)} %w_ref.1) | copy-start | bytes 1179652
  71.0 19.4 %copy-start.1 = (f32[256]{0:T(256)S(1)}, f32[256]{0:T(256)}, u32[]{:S(2)}) copy-start(f32[256]{0:T(256)} %param.8) | copy-start | bytes 3076

commit v4 on v3

--- a/solution.py
+++ b/solution.py
@@ -15,7 +15,8 @@
 LANES = 128
 ROW_STEP = 64
 PER_STEP = 2
-GROUPS = {64: 8, 128: 4, 192: 1, 256: 2}
+GROUPS = {64: 8, 128: 4, 192: 1, 256: 1}
+ORDER = {64: (1, 0), 128: (1, 0), 192: (2, 1), 256: (2, 1)}
 PIECES = 64
 PIECE_ROWS = 32
 
@@ -60,20 +61,19 @@
         grad_prob = [dot_nn(values[:, span(head)], grad_attn_t[span(head), :]) for head in heads]
         return jnp.concatenate(scores, axis=1), jnp.concatenate(grad_prob, axis=1)
 
-    attended, grad_query, grad_key, grad_value = [], [], [], []
-    ready = products(0)
-    for start in range(0, HEADS, size):
-        scores, grad_prob = ready
-        if start + size < HEADS:
-            ready = products(start + size)
+    def soften(scores, grad_prob):
         last = jnp.where(active[-ROW_STEP:], scores[-ROW_STEP:], -1e30)
         scores = jnp.concatenate([scores[:-ROW_STEP], last], axis=0) if rows > ROW_STEP else last
         highest = jnp.max(scores, axis=0, keepdims=True)
         exponent = jnp.exp2((scores - highest) * log_factor)
         probability = exponent * (1.0 / jnp.sum(exponent, axis=0, keepdims=True))
-        prob_group = probability.astype(half)
         row_sum = jnp.sum(probability * grad_prob, axis=0, keepdims=True)
-        score_group = (probability * (grad_prob - row_sum) * factor).astype(half)
+        grad_score = probability * (grad_prob - row_sum) * factor
+        return probability.astype(half), grad_score.astype(half)
+
+    attended, grad_query, grad_key, grad_value = [], [], [], []
+
+    def outputs(start, prob_group, score_group):
         for index in range(size):
             head = start + index
             prob_half = prob_group[:, index * rows : (index + 1) * rows]
@@ -82,6 +82,19 @@
             grad_value.append(dot_nt(grad_attn_t[span(head), :], prob_half).astype(half))
             grad_query.append(dot_nn(keys_t[span(head), :], grad_score).astype(half))
             grad_key.append(dot_nt(queries_t[span(head), :], grad_score).astype(half))
+
+    look, delay = ORDER[rows]
+    starts = list(range(0, HEADS, size))
+    ready = [products(start) for start in starts[:look]]
+    waiting = []
+    for place_in, start in enumerate(starts):
+        if place_in + look < len(starts):
+            ready.append(products(starts[place_in + look]))
+        waiting.append((start, *soften(*ready.pop(0))))
+        if len(waiting) > delay:
+            outputs(*waiting.pop(0))
+    for entry in waiting:
+        outputs(*entry)
     grad_proj_t = jnp.concatenate([*grad_query, *grad_key, *grad_value], axis=0)
     grad_hidden = dot_nn(grad_proj_t.T, wqkv_t_ref[...])
     sum_ref[: 3 * features, :] += dot_nn(grad_proj_t, hidden)

time: 91.8 us -> 89.7 us (0.977)
  blocking collectives: 78.5 us -> 69.4 us
  Pallas kernels: 12.4 us -> 19.6 us
    pallas_call x1, Pallas kernels: 11.1 us -> 18.3 us  [local_grads(): pl.pallas_call(kernel, grid_spec=pltpu.PrefetchScalarGridSpec(num_scalar_...]
    all_to_all x1, blocking collectives: 30.4 us -> 23.5 us  [per_device(): received = lax.all_to_all(send, block, 0, 0)]
    all_to_all x1, blocking collectives: 28.7 us -> 26.5 us  [per_device(): lax.all_to_all(copies, 'z_hi', 0, 0)]
where the time goes in v4:
time: 89.7 us; the launch traced here: 89.6 us
  blocking collectives  69.4 us (77%)
  Pallas kernels  19.6 us (22%)
    all_to_all x1, blocking collectives, per_device(): lax.all_to_all(copies, 'z_hi', 0, 0)  26.5 us
    all_to_all x1, blocking collectives, per_device(): received = lax.all_to_all(send, block, 0, 0)  23.5 us
    all_to_all x1, blocking collectives, per_device(): lax.all_to_all(copies, block, 0, 0)  19.4 us
    pallas_call x1, Pallas kernels, local_grads(): pl.pallas_call(kernel, grid_spec=pltpu.PrefetchScalarGridSpec(num_scalar_...  18.3 us

profile of v4, /device:TPU:1, one launch (start us, length us, event | category | flops | bytes accessed | tf_op | source)
XLA Modules:
  0.0 89.6 jit_solution(14036890243917634176)
XLA Ops:
  0.6 18.3 %window_grads.1 = (bf16[8,256,256]{2,1,0:T(8,128)(2,1)}, bf16[64,32,128]{2,1,0:T(8,128)(2,1)S(1)}) custom-call(s32[1,32]{1,0:T(1,128)} %counts_ref.1, bf16[8,256,256]{2,1,0:T(8,128)(2,1)} %bitcast.7, bf16[8,256,256]{2,1,0:T(8,128)(2,1)} %bitcast.8, f32[1,256]{1,0:T(1,128)} %bitcast.5, bf16[256,768]{1,0:T(8,128)(2,1)} %w_ref.1, bf16[256,256]{1,0:T(8,128)(2,1)} %wout_ref.1), custom_call_target="tpu_custom_call" | custom-call | tf_op jit(solution)/shard_map/window_grads/pallas_call | solution.py:165
  18.9 23.5 %all_to_all.15.in_ref = bf16[64,32,128]{2,1,0:T(8,128)(2,1)S(1)} all-to-all(bf16[64,32,128]{2,1,0:T(8,128)(2,1)S(1)} %get-tuple-element.10), channel_id=1, replica_groups=mesh['z_hi'=8,'z_lo'=2,'core'=2,'help'=4,'dp'=4] {'z_lo','core','help','..., dimensions={0} | all-to-all | bytes 1048576 | tf_op jit(solution)/shard_map/all_to_all | solution.py:270
  42.4 0.1 sum_copies.2
  42.5 26.5 %all_to_all.16.in_ref = f32[8,32,128]{2,1,0:T(8,128)S(1)} all-to-all(f32[8,32,128]{2,1,0:T(8,128)S(1)} %sum_copies.2), channel_id=1, replica_groups=mesh['z_hi'=8,'z_lo'=2,'core'=2,'help'=4,'dp'=4] {'z_hi'}, dimensions={0} | all-to-all | bytes 262144 | tf_op jit(solution)/shard_map/all_to_all | solution.py:272
  69.1 0.0 copy-start
  69.1 0.0 copy-start.1
  69.1 19.4 %all_to_all.17.in_ref = bf16[64,32,128]{2,1,0:T(8,128)(2,1)S(1)} all-to-all(bf16[64,32,128]{2,1,0:T(8,128)(2,1)S(1)} %sum_copies.3), channel_id=1, replica_groups=mesh['z_hi'=8,'z_lo'=2,'core'=2,'help'=4,'dp'=4] {'z_lo','core','help','..., dimensions={0} | all-to-all | bytes 1048576 | tf_op jit(solution)/shard_map/all_to_all | solution.py:273
  88.5 0.0 copy-done
  88.5 0.0 copy-done.1
  88.5 1.1 %unpack.1 = (f32[256,768]{1,0:T(8,128)}, f32[256,256]{1,0:T(8,128)}, f32[1,256]{1,0:T(1,128)}) custom-call(bf16[64,32,128]{2,1,0:T(8,128)(2,1)S(1)} %all_to_all.17.in_ref, bf16[256,768]{1,0:T(8,128)(2,1)S(1)} %copy-done, f32[1,256]{1,0:T(1,128)S(1)} %bitcast.6), custom_call_target="tpu_custom_call" | custom-call | tf_op jit(solution)/shard_map/unpack/pallas_call | solution.py:236
  (1 shorter events, 0.0 us)
Async XLA Ops:
  69.1 19.4 %copy-start = (bf16[256,768]{1,0:T(8,128)(2,1)S(1)}, bf16[256,768]{1,0:T(8,128)(2,1)}, u32[]{:S(2)}) copy-start(bf16[256,768]{1,0:T(8,128)(2,1)} %w_ref.1) | copy-start | bytes 1179652
  69.1 19.4 %copy-start.1 = (f32[256]{0:T(256)S(1)}, f32[256]{0:T(256)}, u32[]{:S(2)}) copy-start(f32[256]{0:T(256)} %param.8) | copy-start | bytes 3076

commit v5 on v4

--- a/solution.py
+++ b/solution.py
@@ -268,7 +268,7 @@
     planes = lax.axis_size("z_hi")
     factor = 1.0 / math.sqrt(planes * lax.axis_size(block) * WKEEP * WIN)
     received = lax.all_to_all(send, block, 0, 0)
-    copies = sum_copies(received, planes, 1.0, jnp.float32)
+    copies = sum_copies(received, planes, 1.0, jnp.bfloat16)
     copies = sum_copies(lax.all_to_all(copies, "z_hi", 0, 0), PIECES, factor, jnp.bfloat16)
     grad_qkv, grad_out, grad_gain = unpack(lax.all_to_all(copies, block, 0, 0), w_qkv, gain)
     grad_tokens = grad_local.reshape(1, slot_count * WIN, features)

time: 89.7 us -> 87.8 us (0.979)
  blocking collectives: 69.4 us -> 67.1 us
    all_to_all x1, blocking collectives: 19.4 us -> 17.8 us  [per_device(): lax.all_to_all(copies, block, 0, 0)]
    all_to_all x1, blocking collectives: 23.5 us -> 22.2 us  [per_device(): received = lax.all_to_all(send, block, 0, 0)]
where the time goes in v5:
time: 87.8 us; the launch traced here: 87.3 us
  blocking collectives  67.1 us (76%)
  Pallas kernels  19.6 us (22%)
    all_to_all x1, blocking collectives, per_device(): lax.all_to_all(copies, 'z_hi', 0, 0)  27.1 us
    all_to_all x1, blocking collectives, per_device(): received = lax.all_to_all(send, block, 0, 0)  22.2 us
    pallas_call x1, Pallas kernels, local_grads(): pl.pallas_call(kernel, grid_spec=pltpu.PrefetchScalarGridSpec(num_scalar_...  18.3 us
    all_to_all x1, blocking collectives, per_device(): lax.all_to_all(copies, block, 0, 0)  17.8 us

profile of v5, /device:TPU:1, one launch (start us, length us, event | category | flops | bytes accessed | tf_op | source)
XLA Modules:
  0.0 87.3 jit_solution(15843106902958837340)
XLA Ops:
  0.6 18.3 %window_grads.1 = (bf16[8,256,256]{2,1,0:T(8,128)(2,1)}, bf16[64,32,128]{2,1,0:T(8,128)(2,1)S(1)}) custom-call(s32[1,32]{1,0:T(1,128)} %counts_ref.1, bf16[8,256,256]{2,1,0:T(8,128)(2,1)} %bitcast.7, bf16[8,256,256]{2,1,0:T(8,128)(2,1)} %bitcast.8, f32[1,256]{1,0:T(1,128)} %bitcast.5, bf16[256,768]{1,0:T(8,128)(2,1)} %w_ref.1, bf16[256,256]{1,0:T(8,128)(2,1)} %wout_ref.1), custom_call_target="tpu_custom_call" | custom-call | tf_op jit(solution)/shard_map/window_grads/pallas_call | solution.py:165
  18.9 22.2 %all_to_all.15.in_ref = bf16[64,32,128]{2,1,0:T(8,128)(2,1)S(1)} all-to-all(bf16[64,32,128]{2,1,0:T(8,128)(2,1)S(1)} %get-tuple-element.10), channel_id=1, replica_groups=mesh['z_hi'=8,'z_lo'=2,'core'=2,'help'=4,'dp'=4] {'z_lo','core','help','..., dimensions={0} | all-to-all | bytes 1048576 | tf_op jit(solution)/shard_map/all_to_all | solution.py:270
  41.1 0.1 sum_copies.2
  41.2 27.1 %all_to_all.16.in_ref = bf16[8,32,128]{2,1,0:T(8,128)(2,1)S(1)} all-to-all(bf16[8,32,128]{2,1,0:T(8,128)(2,1)S(1)} %sum_copies.2), channel_id=1, replica_groups=mesh['z_hi'=8,'z_lo'=2,'core'=2,'help'=4,'dp'=4] {'z_hi'}, dimensions={0} | all-to-all | bytes 131072 | tf_op jit(solution)/shard_map/all_to_all | solution.py:272
  68.3 0.0 copy-start
  68.4 0.0 copy-start.1
  68.4 17.8 %all_to_all.17.in_ref = bf16[64,32,128]{2,1,0:T(8,128)(2,1)S(1)} all-to-all(bf16[64,32,128]{2,1,0:T(8,128)(2,1)S(1)} %sum_copies.3), channel_id=1, replica_groups=mesh['z_hi'=8,'z_lo'=2,'core'=2,'help'=4,'dp'=4] {'z_lo','core','help','..., dimensions={0} | all-to-all | bytes 1048576 | tf_op jit(solution)/shard_map/all_to_all | solution.py:273
  86.2 0.0 copy-done
  86.2 0.0 copy-done.1
  86.2 1.1 %unpack.1 = (f32[256,768]{1,0:T(8,128)}, f32[256,256]{1,0:T(8,128)}, f32[1,256]{1,0:T(1,128)}) custom-call(bf16[64,32,128]{2,1,0:T(8,128)(2,1)S(1)} %all_to_all.17.in_ref, bf16[256,768]{1,0:T(8,128)(2,1)S(1)} %copy-done, f32[1,256]{1,0:T(1,128)S(1)} %bitcast.6), custom_call_target="tpu_custom_call" | custom-call | tf_op jit(solution)/shard_map/unpack/pallas_call | solution.py:236
  (1 shorter events, 0.0 us)
Async XLA Ops:
  68.3 17.8 %copy-start = (bf16[256,768]{1,0:T(8,128)(2,1)S(1)}, bf16[256,768]{1,0:T(8,128)(2,1)}, u32[]{:S(2)}) copy-start(bf16[256,768]{1,0:T(8,128)(2,1)} %w_ref.1) | copy-start | bytes 1179652
  68.4 17.8 %copy-start.1 = (f32[256]{0:T(256)S(1)}, f32[256]{0:T(256)}, u32[]{:S(2)}) copy-start(f32[256]{0:T(256)} %param.8) | copy-start | bytes 3076
